TPU v7x, 256 devices: a whole 4x4x8 slice. The times are simulated.
256 devices in a mesh: dp: 16 (over y, x_lo, core), feat: 16 (over x_hi, z).
Axes of the slice: x: 4 (x_hi: 2, x_lo: 2; x = x_hi * 2 + x_lo), y: 4, z: 8, core: 2. Of those that a mesh axis runs over, the one named last changes fastest.
Arguments:
- samples: bfloat16 [12288, 256], P('dp'), may hold values from -6 to 6
- targets: bfloat16 [12288], P('dp'), may hold values from -6 to 6
- counts: int32 [16], replicated, may hold values from 1 to 768, 6144 in all
- bucket_ids: int32 [3, 256], replicated, may hold values from 0 to 4095
- sign_bits: int32 [3, 256], replicated, may hold values from 0 to 1
Outputs:
- gram: float32 [4096, 4096], P('dp', 'feat')
- zty: float32 [4096], P('feat')
Inputs may be any that keep to these rules, and one draw needn't show every extreme that they name: The counts sum to 6144, and some index of dp has exactly 768 live rows.
All inputs are finite; a program needn't handle non-finite values.
Results may differ from a plain program's by a relative error of at most 0.0048.
Values may be sent and summed in bfloat16 or wider, within the bound.
A program may use at most 64 MiB of HBM per device.

v0:
```python
import math
import jax
import jax.numpy as jnp
from jax import lax
from jax.sharding import PartitionSpec as P

DIN = 256
SK = 4096
BAL_DEV = 384


def inverse_terms(spectra_pair, freq_ids, column_ids):
    turns = freq_ids[:, None] * column_ids[None, :] % SK
    angles = turns.astype(jnp.float32) * (2.0 * math.pi / SK)
    cosine = jnp.cos(angles).astype(jnp.bfloat16)
    sine = jnp.sin(angles).astype(jnp.bfloat16)
    first_term = jnp.einsum(
        "fc,rf->cr", cosine, spectra_pair[0], preferred_element_type=jnp.float32
    )
    second_term = jnp.einsum("fc,rf->cr", sine, spectra_pair[1], preferred_element_type=jnp.float32)
    return first_term - second_term


def complex_times(real_a, imag_a, real_b, imag_b):
    return (real_a * real_b - imag_a * imag_b, real_a * imag_b + imag_a * real_b)


def body(samples, targets, counts, bucket_ids, sign_bits):
    device_row = lax.axis_index("dp")
    local_count = counts[device_row]
    live_mask = (jnp.arange(samples.shape[0], dtype=jnp.int32) < local_count).astype(jnp.float32)
    values = samples.astype(jnp.float32)
    normed = (
        values
        * lax.rsqrt(jnp.mean(values * values, axis=-1, keepdims=True) + 1e-06)
        * DIN ** (-0.5)
    )
    normed = normed * live_mask[:, None]
    freq_panel = SK // lax.axis_size("feat")
    own_ids = lax.axis_index("feat") * freq_panel + jnp.arange(freq_panel, dtype=jnp.int32)
    turns = bucket_ids[:, :, None] * own_ids[None, None, :] % SK
    angles = turns.astype(jnp.float32) * (2.0 * math.pi / SK)
    signed = (2 * sign_bits - 1).astype(jnp.float32)[:, :, None]
    table = jnp.stack([signed * jnp.cos(angles), -signed * jnp.sin(angles)], axis=1)
    table = jnp.transpose(table, (2, 0, 1, 3)).reshape(DIN, 6 * freq_panel)
    spectrum_all = jnp.dot(
        normed, table, precision=lax.Precision.HIGHEST, preferred_element_type=jnp.float32
    )
    spectrum_all = spectrum_all.reshape(normed.shape[0], 3, 2, freq_panel)
    real_mix, imag_mix = complex_times(
        spectrum_all[:, 0, 0], spectrum_all[:, 0, 1], spectrum_all[:, 1, 0], spectrum_all[:, 1, 1]
    )
    real_mix, imag_mix = complex_times(
        real_mix, imag_mix, spectrum_all[:, 2, 0], spectrum_all[:, 2, 1]
    )
    spectra_pair = jnp.stack([real_mix.astype(jnp.bfloat16), imag_mix.astype(jnp.bfloat16)], axis=0)
    portion = lax.all_gather(spectra_pair, "feat", axis=2, tiled=True)
    freq_ids = jnp.arange(portion.shape[2], dtype=jnp.int32)
    summed = inverse_terms(portion, freq_ids, own_ids)
    features = (summed * SK ** (-0.5)).astype(jnp.bfloat16)
    partial_gram = lax.dot_general(
        lax.all_gather(features, "feat", axis=0, tiled=True),
        features,
        (((1,), (1,)), ((), ())),
        preferred_element_type=jnp.float32,
    )
    gram_local = lax.psum_scatter(partial_gram, "dp", scatter_dimension=0, tiled=True)
    target_part = lax.dot_general(
        features, targets, (((1,), (0,)), ((), ())), preferred_element_type=jnp.float32
    )
    target_sum = lax.psum(target_part, "dp")
    total_rows = BAL_DEV * lax.axis_size("dp")
    return (gram_local / total_rows, target_sum * total_rows ** (-0.5))


def solution(mesh):
    placed = (P("dp", None), P("dp"), P(), P(), P())
    return jax.shard_map(
        body, mesh=mesh, in_specs=placed, out_specs=(P("dp", "feat"), P("feat")), check_vma=False
    )
```

profile of v0, /device:TPU:4, one launch (start us, length us, event | category | flops | bytes accessed | tf_op | source)
XLA Modules:
  0.0 457.0 jit_solution(16290275978402960558)
XLA Ops:
  7.2 0.0 all-gather.3.cloned.1.call-start
  7.2 0.7 add_convert_fusion.1
  7.9 0.7 fusion.37
  8.6 1.2 fusion.16
  9.8 1.2 dynamic_slice.3
  11.0 0.6 add_rsqrt_fusion
  11.7 3.9 cosine_multiply_fusion
  15.6 5.2 %fusion.10 = f32[768,3,2,256]{3,0,2,1:T(8,128)S(1)} fusion(f32[3,1,256,256]{2,3,1,0:T(8,128)S(1)} %get-tuple-element.6, f32[3,1,256,256]{2,3,1,0:T(8,128)S(1)} %get-tuple-element.5, bf16[768,256]{1,0:T(8,128)(2,1)} %param.5, f32[768]{0:T(1024)S(1)} %get-tuple-element.8, f32[768]{0:T(1024)S(1)} %get-tuple-element.7), kind=kOutput, calls=%fused_computation.16 | convolution fusion | flops 3624861696 | bytes 6690816 | tf_op jit(solution)/shard_map/dot_general | solution.py:46
  20.8 0.3 fusion.23
  21.1 0.2 fusion.24
  21.4 1.0 pad_maximum_fusion
  22.4 0.0 all-gather.3.cloned.1.call-update
  22.4 0.0 all-gather.5.cloned.1.call-start
  22.5 193.3 %all-gather.3.cloned.1.call-done = bf16[2,768,4096]{2,1,0:T(8,128)(2,1)} async-done(((bf16[2,768,256]{2,1,0:T(8,128)(2,1)}), bf16[2,768,4096]{2,1,0:T(8,128)(2,1)}) %all-gather.3.cloned.1.call-update) | async-done | bytes 12582928 | tf_op jit(solution)/shard_map/all_gather | solution.py:57
  215.7 0.0 copy-start.2
  215.7 21.5 %fusion = f32[256,768]{1,0:T(8,128)S(1)} fusion(bf16[2,768,4096]{2,1,0:T(8,128)(2,1)} %all-gather.3.cloned.1.call-done, s32[256]{0:T(256)S(1)} %iota_add_fusion), kind=kOutput, calls=%fused_computation.1 | convolution fusion | flops 1626341376 | bytes 7078912 | tf_op jit(solution)/shard_map/fc,rf->cr/dot_general | solution.py:20
  237.2 0.0 copy-done.2
  237.2 21.1 %fusion.15 = bf16[256,768]{1,0:T(8,128)(2,1)} fusion(f32[256,768]{1,0:T(8,128)S(1)} %fusion, bf16[2,768,4096]{2,1,0:T(8,128)(2,1)S(1)} %copy-done.2, s32[256]{0:T(256)S(1)} %iota_add_fusion), kind=kOutput, calls=%fused_computation.24 | convolution fusion | flops 1626931200 | bytes 7472128 | tf_op jit(solution)/shard_map/fc,rf->cr/dot_general | solution.py:17
  258.3 0.0 all-gather.5.cloned.1.call-update
  258.3 0.0 reduce-scatter.2.cloned.1.call-start
  258.4 111.3 %all-gather.5.cloned.1.call-done = bf16[4096,768]{1,0:T(8,128)(2,1)} async-done(((bf16[256,768]{1,0:T(8,128)(2,1)}), bf16[4096,768]{1,0:T(8,128)(2,1)}) %all-gather.5.cloned.1.call-update) | async-done | bytes 6291472 | tf_op jit(solution)/shard_map/all_gather | solution.py:62
  369.7 6.7 %fusion.38 = f32[4096,256]{1,0:T(8,128)} fusion(bf16[4096,768]{1,0:T(8,128)(2,1)} %all-gather.5.cloned.1.call-done, bf16[256,768]{1,0:T(8,128)(2,1)} %fusion.15), kind=kOutput, calls=%fused_computation.63 | convolution fusion | flops 1610612736 | bytes 10878976 | tf_op jit(solution)/shard_map/dot_general | solution.py:61
  376.3 0.0 copy-start.1
  376.3 0.0 copy-start
  376.3 0.0 reduce-scatter.2.cloned.1.call-update
  376.4 0.7 copy-done.1
  377.0 0.3 copy-done
  377.3 0.2 fusion.39
  377.5 29.4 %psum.7 = f32[256]{0:T(256)S(1)} all-reduce(f32[256]{0:T(256)S(1)} %bitcast.36), channel_id=1, replica_groups=mesh['dp'=16,'feat'=16] {'dp'}, use_global_device_ids=true, to_apply=%region_2.3 | all-reduce | flops 256 | bytes 2048 | tf_op jit(solution)/shard_map/psum | solution.py:71
  406.9 0.6 broadcast_multiply_fusion.1
  407.5 41.3 %reduce-scatter.2.cloned.1.call-done = f32[256,256]{1,0:T(8,128)} async-done(((f32[4096,256]{1,0:T(8,128)}), f32[256,256]{1,0:T(8,128)}) %reduce-scatter.2.cloned.1.call-update) | async-done | bytes 262160 | tf_op jit(solution)/shard_map/reduce_scatter | solution.py:67
  448.8 1.7 broadcast_multiply_fusion
  (2 shorter events, 0.0 us)
Async XLA Ops:
  7.2 208.6 %all-gather.3.cloned.1.call-start = ((), (), s32[]{:S(2)}) async-start(), calls=%async_computation.1 | async-start | bytes 13369344 | tf_op jit(solution)/shard_map/all_gather | solution.py:57
  22.4 347.3 %all-gather.5.cloned.1.call-start = ((), (), s32[]{:S(2)}) async-start(), calls=%async_computation.2 | async-start | bytes 6684672 | tf_op jit(solution)/shard_map/all_gather | solution.py:62
  215.7 21.5 %copy-start.2 = (bf16[2,768,4096]{2,1,0:T(8,128)(2,1)S(1)}, bf16[2,768,4096]{2,1,0:T(8,128)(2,1)}, u32[]{:S(2)}) copy-start(bf16[2,768,4096]{2,1,0:T(8,128)(2,1)} %all-gather.3.cloned.1.call-done) | copy-start | bytes 37748740
  258.3 190.5 %reduce-scatter.2.cloned.1.call-start = ((), (), s32[]{:S(2)}) async-start(), calls=%async_computation.3 | async-start | bytes 4456448 | tf_op jit(solution)/shard_map/reduce_scatter | solution.py:67
  376.3 0.7 copy-start.1
  376.3 1.0 copy-start
Sparse Core Ops, SparseCore 0:
  22.5 193.1 all-gather.2
  258.5 111.1 all-gather.4
  376.5 72.3 reduce-scatter.1
where the time goes:
time: 457 us
  waiting for transfers between devices  346 us (76%)
  matrix products  54.6 us (12%)
  blocking collectives  29.4 us (6%)
  between operations  13.8 us (3%)
  other arithmetic  10.9 us (2%)
    all_gather x1, waiting for transfers between devices, body(): portion = lax.all_gather(spectra_pair, 'feat', axis=2, tiled=True)  193 us
    all_gather x1, waiting for transfers between devices, body(): lax.all_gather(features, 'feat', axis=0, tiled=True)  111 us
    reduce_scatter x1, waiting for transfers between devices, body(): lax.psum_scatter(partial_gram, 'dp', scatter_dimension=0, tiled=True)  41.3 us
    psum x1, blocking collectives, body(): target_sum = lax.psum(target_part, 'dp')  29.4 us
    dot_general x1, matrix products, inverse_terms(): jnp.einsum('fc,rf->cr', sine, spectra_pair[1], preferred_element_type=jnp...  21.5 us
    dot_general x1, matrix products, inverse_terms(): jnp.einsum('fc,rf->cr', cosine, spectra_pair[0], preferred_element_type=j...  21.1 us
  transfers between devices with their start and end apart: 3, of which 3 were waited for; matrix products, arithmetic and copies ran while one was open for 0% of the time, Pallas kernels for 0%

commit v1 on v0

--- a/solution.py
+++ b/solution.py
@@ -54,7 +54,8 @@
         real_mix, imag_mix, spectrum_all[:, 2, 0], spectrum_all[:, 2, 1]
     )
     spectra_pair = jnp.stack([real_mix.astype(jnp.bfloat16), imag_mix.astype(jnp.bfloat16)], axis=0)
-    portion = lax.all_gather(spectra_pair, "feat", axis=2, tiled=True)
+    outgoing = jnp.stack([spectra_pair] * lax.axis_size("feat"))
+    portion = jnp.concatenate(lax.all_to_all(outgoing, "feat", 0, 0), axis=2)
     freq_ids = jnp.arange(portion.shape[2], dtype=jnp.int32)
     summed = inverse_terms(portion, freq_ids, own_ids)
     features = (summed * SK ** (-0.5)).astype(jnp.bfloat16)

time: 457 us -> 556 us (1.22); the launches traced: 457 us -> 549 us
  blocking collectives: 29.4 us -> 314 us
  waiting for transfers between devices: 346 us -> 153 us
  local copies, waits for them, and re-layouts: 2.23 us -> 11.9 us
  matrix products: 54.6 us -> 45 us
    all_to_all x0 -> x1, blocking collectives: none -> 284 us  [body(): portion = jnp.concatenate(lax.all_to_all(outgoing, 'feat', 0, 0), axis=2)]
    all_gather x1 -> x0, waiting for transfers between devices: 193 us -> none  [body(): portion = lax.all_gather(spectra_pair, 'feat', axis=2, tiled=True)]
    another operation x0 -> x2, local copies, waits for them, and re-layouts: none -> 6.24 us  [the longest x1 5.97 us: body(): outgoing = jnp.stack([spectra_pair] * lax.axis_size('feat'))]
  transfers between devices with their start and end apart: 3 -> 2, of which waited for: 3 -> 2; matrix products, arithmetic and copies ran while one was open for 0% -> 0% of each run, Pallas kernels for 0% -> 0%
where the time goes in v1:
time: 556 us; the launch traced here: 549 us
  blocking collectives  314 us (56%)
  waiting for transfers between devices  153 us (28%)
  matrix products  45 us (8%)
  between operations  14.5 us (3%)
  local copies, waits for them, and re-layouts  11.9 us (2%)
  other arithmetic  9.97 us (2%)
    all_to_all x1, blocking collectives, body(): portion = jnp.concatenate(lax.all_to_all(outgoing, 'feat', 0, 0), axis=2)  284 us
    all_gather x1, waiting for transfers between devices, body(): lax.all_gather(features, 'feat', axis=0, tiled=True)  112 us
    reduce_scatter x1, waiting for transfers between devices, body(): lax.psum_scatter(partial_gram, 'dp', scatter_dimension=0, tiled=True)  41.4 us
    psum x1, blocking collectives, body(): target_sum = lax.psum(target_part, 'dp')  29.4 us
    dot_general x1, matrix products, inverse_terms(): jnp.einsum('fc,rf->cr', sine, spectra_pair[1], preferred_element_type=jnp...  17 us
    dot_general x1, matrix products, inverse_terms(): jnp.einsum('fc,rf->cr', cosine, spectra_pair[0], preferred_element_type=j...  16 us
  transfers between devices with their start and end apart: 2, of which 2 were waited for; matrix products, arithmetic and copies ran while one was open for 0% of the time, Pallas kernels for 0%

profile of v1, /device:TPU:4, one launch (start us, length us, event | category | flops | bytes accessed | tf_op | source)
XLA Modules:
  0.0 548.7 jit_solution(1466950316680845276)
XLA Ops:
  7.2 0.0 all-gather.2.cloned.1.call-start
  7.2 0.7 add_convert_fusion.1
  7.9 0.7 fusion.37
  8.6 1.2 fusion.16
  9.8 1.2 dynamic_slice.3
  11.0 0.6 add_rsqrt_fusion
  11.7 3.9 cosine_multiply_fusion
  15.6 5.2 fusion.10
  20.8 0.3 fusion.23
  21.1 0.2 fusion.24
  21.4 0.1 pad_maximum_fusion
  21.5 0.3 copy.8
  21.7 6.0 %stack.8 = bf16[16,2,768,256]{2,3,1,0:T(8,128)(2,1)} broadcast(bf16[2,768,256]{1,2,0:T(8,128)(2,1)S(1)} %copy.8), dimensions={1,2,3} | broadcast | bytes 13369344 | tf_op jit(solution)/shard_map/stack | solution.py:57
  27.7 284.3 %all_to_all.5 = bf16[16,2,768,256]{2,3,1,0:T(8,128)(2,1)S(1)} all-to-all(bf16[16,2,768,256]{2,3,1,0:T(8,128)(2,1)} %stack.8), channel_id=1, replica_groups=mesh['dp'=16,'feat'=16] {'feat'}, dimensions={0} | all-to-all | bytes 25165824 | tf_op jit(solution)/shard_map/all_to_all | solution.py:58
  312.0 1.9 copy.12
  314.0 1.5 fusion.38
  315.5 16.0 %fusion.6 = f32[256,768]{1,0:T(8,128)S(1)} fusion(bf16[768,4096]{0,1:T(8,128)(2,1)S(1)} %bitcast.33, s32[256]{0:T(256)S(1)} %iota_add_fusion), kind=kOutput, calls=%fused_computation.12 | convolution fusion | flops 1626341376 | bytes 7078912 | tf_op jit(solution)/shard_map/fc,rf->cr/dot_general | solution.py:17
  331.5 17.0 %fusion.15 = bf16[256,768]{1,0:T(8,128)(2,1)} fusion(f32[256,768]{1,0:T(8,128)S(1)} %fusion.6, bf16[768,4096]{0,1:T(8,128)(2,1)S(1)} %bitcast.32, s32[256]{0:T(256)S(1)} %iota_add_fusion), kind=kOutput, calls=%fused_computation.23 | convolution fusion | flops 1626931200 | bytes 7472128 | tf_op jit(solution)/shard_map/fc,rf->cr/dot_general | solution.py:20
  348.5 0.0 all-gather.2.cloned.1.call-update
  348.5 0.0 reduce-scatter.2.cloned.1.call-start
  348.6 112.0 %all-gather.2.cloned.1.call-done = bf16[4096,768]{1,0:T(8,128)(2,1)} async-done(((bf16[256,768]{1,0:T(8,128)(2,1)}), bf16[4096,768]{1,0:T(8,128)(2,1)}) %all-gather.2.cloned.1.call-update) | async-done | bytes 6291472 | tf_op jit(solution)/shard_map/all_gather | solution.py:63
  460.6 6.7 %fusion.39 = f32[4096,256]{1,0:T(8,128)} fusion(bf16[4096,768]{1,0:T(8,128)(2,1)} %all-gather.2.cloned.1.call-done, bf16[256,768]{1,0:T(8,128)(2,1)} %fusion.15), kind=kOutput, calls=%fused_computation.63 | convolution fusion | flops 1610612736 | bytes 10878976 | tf_op jit(solution)/shard_map/dot_general | solution.py:62
  467.3 0.0 copy-start.1
  467.3 0.0 copy-start
  467.3 0.0 reduce-scatter.2.cloned.1.call-update
  467.3 0.7 copy-done.1
  467.9 0.3 copy-done
  468.3 0.2 fusion.40
  468.4 29.4 %psum.7 = f32[256]{0:T(256)S(1)} all-reduce(f32[256]{0:T(256)S(1)} %bitcast.34), channel_id=1, replica_groups=mesh['dp'=16,'feat'=16] {'dp'}, use_global_device_ids=true, to_apply=%region_2.3 | all-reduce | flops 256 | bytes 2048 | tf_op jit(solution)/shard_map/psum | solution.py:72
  497.9 0.6 broadcast_multiply_fusion.1
  498.4 41.4 %reduce-scatter.2.cloned.1.call-done = f32[256,256]{1,0:T(8,128)} async-done(((f32[4096,256]{1,0:T(8,128)}), f32[256,256]{1,0:T(8,128)}) %reduce-scatter.2.cloned.1.call-update) | async-done | bytes 262160 | tf_op jit(solution)/shard_map/reduce_scatter | solution.py:68
  539.8 1.7 broadcast_multiply_fusion
  (2 shorter events, 0.0 us)
Async XLA Ops:
  7.2 453.4 %all-gather.2.cloned.1.call-start = ((), (), s32[]{:S(2)}) async-start(), calls=%async_computation.2 | async-start | bytes 6684672 | tf_op jit(solution)/shard_map/all_gather | solution.py:63
  348.5 191.3 %reduce-scatter.2.cloned.1.call-start = ((), (), s32[]{:S(2)}) async-start(), calls=%async_computation.3 | async-start | bytes 4456448 | tf_op jit(solution)/shard_map/reduce_scatter | solution.py:68
  467.3 0.7 copy-start.1
  467.3 1.0 copy-start
Sparse Core Ops, SparseCore 0:
  348.6 111.9 all-gather.1
  467.4 72.3 reduce-scatter.1
